TPU v7x, 256 devices: a whole 4x4x8 slice. The times are simulated.
256 devices in a mesh: rows: 32 (over x, z), vecs: 8 (over y, core).
Axes of the slice: x: 4, y: 4, z: 8, core: 2. Of those that a mesh axis runs over, the one named last changes fastest.
Arguments:
- coords: float32 [3, 8192], P(None, ('rows', 'vecs')), may hold values from 0 to 1
- old_vectors: bfloat16 [8192, 16384], P('rows', 'vecs'), may hold values from -0.078125 to 0.078125
- pivots: int32 [2, 128], replicated, may hold values from 0 to 8191, as said below
- slots: int32 [8192], replicated, may hold values from 0 to 8191, each once
Outputs:
- new_vectors: float32 [8192, 256], P(('rows', 'vecs'))
Inputs may be any that keep to these rules, and one draw needn't show every extreme that they name: `pivots`: all 256 pivot numbers are distinct. `slots`: each window row belongs to exactly one point.
All inputs are finite; a program needn't handle non-finite values.
Results may differ from a plain program's by a relative error of at most 0.0003.
Values may be sent and summed in bfloat16 or wider, within the bound.
A program may use at most 64 MiB of HBM per device.

v0:
```python
import jax
import jax.numpy as jnp
from jax import lax
from jax.sharding import PartitionSpec as P

length_scale = 0.5
noise_shift = 12.0


def matern(points, centers):
    dist_sq = jnp.zeros((points.shape[1], centers.shape[1]), jnp.float32)
    for component in range(3):
        differ = points[component][:, None] - centers[component][None, :]
        dist_sq = dist_sq + differ * differ
    scaled = jnp.sqrt(5.0 * dist_sq) / length_scale
    return (1.0 + scaled + scaled * scaled / 3.0) * jnp.exp(-scaled)


def pick_rows(block_data, wanted, first_row):
    length = block_data.shape[0]
    offset = wanted - first_row
    inside = (offset >= 0) & (offset < length)
    bounded = jnp.clip(offset, 0, length - 1)
    fetched = jnp.take(block_data, bounded, axis=0)
    return jnp.where(inside[:, None], fetched, jnp.zeros((), block_data.dtype))


def shards(coords, old_vectors, pivots, slots):
    row_block = old_vectors.shape[0]
    share = coords.shape[1]
    panels = pivots.shape[0]
    width = pivots.shape[1]
    block_first = lax.axis_index("rows") * row_block
    share_first = block_first + lax.axis_index("vecs") * share
    wanted = jnp.take(slots, pivots.reshape(-1), axis=0)
    my_rows = share_first + jnp.arange(share, dtype=jnp.int32)
    every_point = lax.all_gather(coords, ("rows", "vecs"), axis=1, tiled=True)
    centers = jnp.take(every_point, wanted, axis=1)
    new_panels = []
    for panel in range(panels):
        chosen = wanted[panel * width : (panel + 1) * width]
        old_pivot = (
            lax.psum(pick_rows(old_vectors, chosen, block_first), "rows")
            .astype(jnp.float32)
            .astype(jnp.bfloat16)
        )

        def residual_term(first_row, length, old_pivot=old_pivot):
            return jnp.dot(old_vectors, old_pivot.T, preferred_element_type=jnp.float32)

        summed = lax.psum_scatter(
            residual_term(jnp.int32(0), share * lax.axis_size("vecs")),
            "vecs",
            scatter_dimension=0,
            tiled=True,
        )
        kernel = matern(coords, centers[:, panel * width : (panel + 1) * width])
        kernel = kernel + noise_shift * (my_rows[:, None] == chosen[None, :]).astype(jnp.float32)
        current = kernel - summed
        if panel > 0:
            stacked = new_panels[0]
            earlier = lax.psum(pick_rows(stacked, chosen, share_first), ("rows", "vecs"))
            current = current - jnp.dot(
                stacked,
                earlier.T,
                precision=lax.Precision.HIGHEST,
                preferred_element_type=jnp.float32,
            )
        block = lax.psum(pick_rows(current, chosen, share_first), ("rows", "vecs"))
        factor = jnp.linalg.cholesky(block)
        fresh = jax.scipy.linalg.solve_triangular(factor, current.T, lower=True).T
        new_panels.append(fresh)
    return jnp.concatenate(new_panels, axis=1)


def solution(mesh):
    in_specs = (P(None, ("rows", "vecs")), P("rows", "vecs"), P(), P())
    out_specs = P(("rows", "vecs"), None)
    return jax.shard_map(shards, mesh=mesh, in_specs=in_specs, out_specs=out_specs, check_vma=False)
```

profile of v0, /device:TPU:1, one launch (start us, length us, event | category | flops | bytes accessed | tf_op | source)
XLA Modules:
  0.0 1000.4 jit_solution(14306244718149790146)
XLA Ops:
  6.5 0.8 compare_select_fusion.1
  7.3 2.0 gather_fusion
  9.3 0.7 compare_and_fusion.7
  10.1 0.9 gather_fusion.4
  11.0 0.9 gather_fusion.2
  12.0 1.2 select_select_fusion
  13.2 73.2 %all-gather = f32[256,32,3]{1,2,0:T(4,128)S(1)} all-gather(f32[1,32,3]{1,2,0:T(4,128)S(1)} %bitcast.66), channel_id=1, replica_groups=mesh['rows'=32,'vecs'=8] {'rows','vecs'}, dimensions={0}, use_global_device_ids=true | all-gather | bytes 98688 | tf_op jit(solution)/shard_map/all_gather | solution.py:37
  86.5 3.0 copy.23
  89.5 2.9 gather_fusion.1
  92.4 0.1 select_bitcast_fusion
  92.5 0.3 slice_reduce_fusion.2
  92.8 70.1 %all-reduce.12.cloned.1.call-done = (bf16[128,2048]{1,0:T(8,128)(2,1)}, bf16[128,2048]{1,0:T(8,128)(2,1)}) async-done(((bf16[128,2048]{1,0:T(8,128)(2,1)}, bf16[128,2048]{1,0:T(8,128)(2,1)}), (bf16[128,2048]{1,0:T(8,128)(2,1)}, bf16[128,2048]{1,0:T(8,128)(2,1)})) %all-reduce.12.cloned.1.call-update) | async-done | bytes 1048592 | tf_op jit(solution)/shard_map/psum | solution.py:43
  162.9 1.5 convolution_bitcast_fusion.1
  164.4 0.7 copy.31
  165.3 33.3 %reduce-scatter.7.cloned.1.call-done = f32[32,128]{1,0:T(8,128)} async-done(((f32[256,128]{1,0:T(8,128)}), f32[32,128]{1,0:T(8,128)}) %reduce-scatter.7.cloned.1.call-update) | async-done | bytes 16400 | tf_op jit(solution)/shard_map/reduce_scatter | solution.py:51
  198.5 0.8 add_subtract_fusion
  199.3 0.6 gather_fusion.3
  200.0 0.1 copy.25
  200.1 0.6 select_select_fusion.6
  200.8 1.5 convolution_bitcast_fusion
  202.3 0.7 copy.33
  203.1 243.7 %all-reduce.6.cloned.1.call-done = f32[128,128]{0,1:T(8,128)} async-done(((f32[128,128]{0,1:T(8,128)}), f32[128,128]{0,1:T(8,128)}) %all-reduce.6.cloned.1.call-update) | async-done | bytes 65552 | tf_op jit(solution)/shard_map/psum | solution.py:69
  446.9 0.9 copy.26
  447.8 0.9 fusion.6
  448.6 11.7 %cholesky.44 = f32[128,128]{1,0:T(8,128)S(1)} custom-call(f32[128,128]{1,0:T(8,128)S(1)} %fusion.6), custom_call_target="Cholesky" | custom-call | tf_op jit(solution)/shard_map/jit(cholesky)/cholesky | solution.py:70
  460.4 0.6 compare_reduce_fusion.1
  461.0 0.7 fusion
  461.7 9.8 custom-call.6
  471.5 0.2 fusion.4
  471.7 0.7 gather_fusion.5
  472.3 0.1 copy.28
  472.4 0.6 select_select_fusion.5
  473.1 0.2 all-reduce.10.cloned.1.call-start
  473.3 3.4 reduce-scatter.9.cloned.1.call-done
  476.7 248.0 %all-reduce.8.cloned.1.call-done = f32[128,128]{0,1:T(8,128)} async-done(((f32[128,128]{0,1:T(8,128)}), f32[128,128]{0,1:T(8,128)}) %all-reduce.8.cloned.1.call-update) | async-done | bytes 65552 | tf_op jit(solution)/shard_map/psum | solution.py:62
  724.8 1.0 convolution_subtract_fusion
  725.8 0.6 gather_fusion.6
  726.5 0.1 copy.29
  726.6 0.6 select_select_fusion.4
  727.2 240.9 %all-reduce.10.cloned.1.call-done = f32[128,128]{0,1:T(8,128)} async-done(((f32[128,128]{0,1:T(8,128)}), f32[128,128]{0,1:T(8,128)}) %all-reduce.10.cloned.1.call-update) | async-done | bytes 65552 | tf_op jit(solution)/shard_map/psum | solution.py:69
  968.1 0.9 copy.30
  969.0 0.9 fusion.3
  969.9 11.7 %cholesky.55 = f32[128,128]{1,0:T(8,128)S(1)} custom-call(f32[128,128]{1,0:T(8,128)S(1)} %fusion.3), custom_call_target="Cholesky" | custom-call | tf_op jit(solution)/shard_map/jit(cholesky)/cholesky | solution.py:70
  981.6 0.6 compare_reduce_fusion
  982.3 0.7 fusion.1
  983.0 9.8 custom-call.7
  992.8 0.2 convolution_bitcast_fusion.2
  992.9 0.6 pad_maximum_fusion
  (30 shorter events, 0.4 us)
Async XLA Ops:
  6.5 3.5 copy-start
  6.5 156.3 %all-reduce.12.cloned.1.call-start = ((), (), s32[]{:S(2)}) async-start(), calls=%async_computation.7 | async-start | bytes 2097152 | tf_op jit(solution)/shard_map/psum | solution.py:43
  11.0 2.2 copy-start.2
  12.0 77.5 %copy-start.1 = (s32[2,128]{1,0:T(2,128)S(1)}, s32[2,128]{1,0:T(2,128)}, u32[]{:S(2)}) copy-start(s32[2,128]{1,0:T(2,128)} %param.13) | copy-start | bytes 3076
  13.2 185.3 %reduce-scatter.7.cloned.1.call-start = ((), (), s32[]{:S(2)}) async-start(), calls=%async_computation.5 | async-start | bytes 147456 | tf_op jit(solution)/shard_map/reduce_scatter | solution.py:51
  165.2 281.7 %all-reduce.6.cloned.1.call-start = ((), (), s32[]{:S(2)}) async-start(), calls=%async_computation.2 | async-start | bytes 131072 | tf_op jit(solution)/shard_map/psum | solution.py:69
  200.7 276.0 %reduce-scatter.9.cloned.1.call-start = ((), (), s32[]{:S(2)}) async-start(), calls=%async_computation.6 | async-start | bytes 147456 | tf_op jit(solution)/shard_map/reduce_scatter | solution.py:51
  203.1 521.7 %all-reduce.8.cloned.1.call-start = ((), (), s32[]{:S(2)}) async-start(), calls=%async_computation.3 | async-start | bytes 131072 | tf_op jit(solution)/shard_map/psum | solution.py:62
  473.1 495.0 %all-reduce.10.cloned.1.call-start = ((), (), s32[]{:S(2)}) async-start(), calls=%async_computation.4 | async-start | bytes 131072 | tf_op jit(solution)/shard_map/psum | solution.py:69
Sparse Core Ops, SparseCore 0:
  13.3 149.5 all-reduce.11
  165.4 33.0 reduce-scatter.6
  204.0 242.7 all-reduce.5
  449.2 27.4 reduce-scatter.8
  482.1 242.6 all-reduce.7
  730.2 237.9 all-reduce.9
where the time goes:
time: 1000 us
  waiting for transfers between devices  840 us (84%)
  blocking collectives  73.2 us (7%)
  other arithmetic  53.6 us (5%)
  local copies, waits for them, and re-layouts  15.6 us (2%)
  between operations  13.7 us (1%)
    psum x2, waiting for transfers between devices, shards(): block = lax.psum(pick_rows(current, chosen, share_first), ('rows', 'vecs'))  485 us
    psum x1, waiting for transfers between devices, shards(): lax.psum(pick_rows(stacked, chosen, share_first), ('rows', 'vecs'))  248 us
    all_gather x1, blocking collectives, shards(): every_point = lax.all_gather(coords, ('rows', 'vecs'), axis=1, tiled=True)  73.2 us
    psum x1, waiting for transfers between devices, shards(): lax.psum(pick_rows(old_vectors, chosen, block_first), 'rows')  70.1 us
    reduce_scatter x2, waiting for transfers between devices, shards(): lax.psum_scatter(residual_term(jnp.int32(0), share * lax.axis_size('vecs'...  36.7 us
    another operation x6, other arithmetic, shards(): factor = jnp.linalg.cholesky(block)  24.8 us
    another operation x4, other arithmetic, shards(): fresh = jax.scipy.linalg.solve_triangular(factor, current.T, lower=True).T  20.9 us
  transfers between devices with their start and end apart: 6, of which 6 were waited for; matrix products, arithmetic and copies ran while one was open for 3% of the time, Pallas kernels for 0%

commit v1 on v0

--- a/solution.py
+++ b/solution.py
@@ -66,7 +66,7 @@
                 precision=lax.Precision.HIGHEST,
                 preferred_element_type=jnp.float32,
             )
-        block = lax.psum(pick_rows(current, chosen, share_first), ("rows", "vecs"))
+        block = lax.psum(lax.psum(pick_rows(current, chosen, share_first), "vecs"), "rows")
         factor = jnp.linalg.cholesky(block)
         fresh = jax.scipy.linalg.solve_triangular(factor, current.T, lower=True).T
         new_panels.append(fresh)

time: 1000 us -> 930 us (0.930)
  waiting for transfers between devices: 840 us -> 765 us
    psum x2 -> x4, waiting for transfers between devices: 485 us -> 404 us  [the longest x2 281 us: shards(): lax.psum(lax.psum(pick_rows(current, chosen, share_first), 'vecs'), 'rows')]
  transfers between devices with their start and end apart: 6 -> 8, of which waited for: 6 -> 8; matrix products, arithmetic and copies ran while one was open for 3% -> 4% of each run, Pallas kernels for 0% -> 0%
where the time goes in v1:
time: 930 us; the launch traced here: 926 us
  waiting for transfers between devices  765 us (82%)
  blocking collectives  73.2 us (8%)
  other arithmetic  53.6 us (6%)
  local copies, waits for them, and re-layouts  15.6 us (2%)
  between operations  13.7 us (1%)
    psum x2, waiting for transfers between devices, shards(): lax.psum(lax.psum(pick_rows(current, chosen, share_first), 'vecs'), 'rows')  281 us
    psum x1, waiting for transfers between devices, shards(): lax.psum(pick_rows(stacked, chosen, share_first), ('rows', 'vecs'))  248 us
    psum x2, waiting for transfers between devices, shards(): lax.psum(pick_rows(current, chosen, share_first), 'vecs')  123 us
    all_gather x1, blocking collectives, shards(): every_point = lax.all_gather(coords, ('rows', 'vecs'), axis=1, tiled=True)  73.2 us
    psum x1, waiting for transfers between devices, shards(): lax.psum(pick_rows(old_vectors, chosen, block_first), 'rows')  70.1 us
    reduce_scatter x2, waiting for transfers between devices, shards(): lax.psum_scatter(residual_term(jnp.int32(0), share * lax.axis_size('vecs'...  43.2 us
    another operation x6, other arithmetic, shards(): factor = jnp.linalg.cholesky(block)  24.8 us
    another operation x4, other arithmetic, shards(): fresh = jax.scipy.linalg.solve_triangular(factor, current.T, lower=True).T  20.9 us
  transfers between devices with their start and end apart: 8, of which 8 were waited for; matrix products, arithmetic and copies ran while one was open for 4% of the time, Pallas kernels for 0%

profile of v1, /device:TPU:1, one launch (start us, length us, event | category | flops | bytes accessed | tf_op | source)
XLA Modules:
  0.0 926.1 jit_solution(4646000098382469093)
XLA Ops:
  6.5 0.8 compare_select_fusion.1
  7.3 2.0 gather_fusion
  9.3 0.7 compare_and_fusion.7
  10.1 0.9 gather_fusion.4
  11.0 0.9 gather_fusion.2
  12.0 1.2 select_select_fusion
  13.2 73.2 %all-gather = f32[256,32,3]{1,2,0:T(4,128)S(1)} all-gather(f32[1,32,3]{1,2,0:T(4,128)S(1)} %bitcast.66), channel_id=1, replica_groups=mesh['rows'=32,'vecs'=8] {'rows','vecs'}, dimensions={0}, use_global_device_ids=true | all-gather | bytes 98688 | tf_op jit(solution)/shard_map/all_gather | solution.py:37
  86.5 3.0 copy.23
  89.5 2.9 gather_fusion.1
  92.4 0.1 select_bitcast_fusion
  92.5 0.3 slice_reduce_fusion.2
  92.8 70.1 %all-reduce.18.cloned.1.call-done = (bf16[128,2048]{1,0:T(8,128)(2,1)}, bf16[128,2048]{1,0:T(8,128)(2,1)}) async-done(((bf16[128,2048]{1,0:T(8,128)(2,1)}, bf16[128,2048]{1,0:T(8,128)(2,1)}), (bf16[128,2048]{1,0:T(8,128)(2,1)}, bf16[128,2048]{1,0:T(8,128)(2,1)})) %all-reduce.18.cloned.1.call-update) | async-done | bytes 1048592 | tf_op jit(solution)/shard_map/psum | solution.py:43
  162.9 1.5 convolution_bitcast_fusion.1
  164.4 0.7 copy.31
  165.3 33.3 %reduce-scatter.7.cloned.1.call-done = f32[32,128]{1,0:T(8,128)} async-done(((f32[256,128]{1,0:T(8,128)}), f32[32,128]{1,0:T(8,128)}) %reduce-scatter.7.cloned.1.call-update) | async-done | bytes 16400 | tf_op jit(solution)/shard_map/reduce_scatter | solution.py:51
  198.5 0.8 add_subtract_fusion
  199.3 0.6 gather_fusion.3
  200.0 0.1 copy.25
  200.1 0.6 select_select_fusion.6
  200.8 64.0 %all-reduce.8.cloned.1.call-done = f32[128,128]{0,1:T(8,128)} async-done(((f32[128,128]{0,1:T(8,128)}), f32[128,128]{0,1:T(8,128)}) %all-reduce.8.cloned.1.call-update) | async-done | bytes 65552 | tf_op jit(solution)/shard_map/psum | solution.py:69
  264.9 1.5 convolution_bitcast_fusion
  266.4 0.7 copy.33
  267.3 139.0 %all-reduce.10.cloned.1.call-done = f32[128,128]{0,1:T(8,128)} async-done(((f32[128,128]{0,1:T(8,128)}), f32[128,128]{0,1:T(8,128)}) %all-reduce.10.cloned.1.call-update) | async-done | bytes 65552 | tf_op jit(solution)/shard_map/psum | solution.py:69
  406.3 0.9 copy.26
  407.2 0.9 fusion.6
  408.1 11.7 %cholesky.44 = f32[128,128]{1,0:T(8,128)S(1)} custom-call(f32[128,128]{1,0:T(8,128)S(1)} %fusion.6), custom_call_target="Cholesky" | custom-call | tf_op jit(solution)/shard_map/jit(cholesky)/cholesky | solution.py:70
  419.8 0.6 compare_reduce_fusion.1
  420.5 0.7 fusion
  421.1 9.8 %custom-call.6 = f32[1,128,128]{1,2,0:T(8,128)S(1)} custom-call(f32[1,128,128]{2,1,0:T(8,128)S(1)} %fusion), custom_call_target="InvertDiagBlocksLowerTriangular" | custom-call | tf_op jit(solution)/shard_map/jit(_solve_triangular)/triangular_solve | solution.py:71
  431.0 0.2 fusion.4
  431.1 0.7 gather_fusion.5
  431.9 0.6 select_select_fusion.5
  432.6 9.9 %reduce-scatter.9.cloned.1.call-done = f32[32,128]{1,0:T(8,128)} async-done(((f32[256,128]{1,0:T(8,128)}), f32[32,128]{1,0:T(8,128)}) %reduce-scatter.9.cloned.1.call-update) | async-done | bytes 16400 | tf_op jit(solution)/shard_map/reduce_scatter | solution.py:51
  442.5 248.1 %all-reduce.12.cloned.1.call-done = f32[128,128]{0,1:T(8,128)} async-done(((f32[128,128]{0,1:T(8,128)}), f32[128,128]{0,1:T(8,128)}) %all-reduce.12.cloned.1.call-update) | async-done | bytes 65552 | tf_op jit(solution)/shard_map/psum | solution.py:62
  690.6 1.0 convolution_subtract_fusion
  691.6 0.6 gather_fusion.6
  692.4 0.6 select_select_fusion.4
  693.0 0.2 all-reduce.16.cloned.1.call-start
  693.2 59.0 %all-reduce.14.cloned.1.call-done = f32[128,128]{0,1:T(8,128)} async-done(((f32[128,128]{0,1:T(8,128)}), f32[128,128]{0,1:T(8,128)}) %all-reduce.14.cloned.1.call-update) | async-done | bytes 65552 | tf_op jit(solution)/shard_map/psum | solution.py:69
  752.2 141.6 %all-reduce.16.cloned.1.call-done = f32[128,128]{0,1:T(8,128)} async-done(((f32[128,128]{0,1:T(8,128)}), f32[128,128]{0,1:T(8,128)}) %all-reduce.16.cloned.1.call-update) | async-done | bytes 65552 | tf_op jit(solution)/shard_map/psum | solution.py:69
  893.8 0.9 copy.30
  894.7 0.9 fusion.3
  895.6 11.7 %cholesky.55 = f32[128,128]{1,0:T(8,128)S(1)} custom-call(f32[128,128]{1,0:T(8,128)S(1)} %fusion.3), custom_call_target="Cholesky" | custom-call | tf_op jit(solution)/shard_map/jit(cholesky)/cholesky | solution.py:70
  907.3 0.6 compare_reduce_fusion
  908.0 0.7 fusion.1
  908.6 9.8 %custom-call.7 = f32[1,128,128]{1,2,0:T(8,128)S(1)} custom-call(f32[1,128,128]{2,1,0:T(8,128)S(1)} %fusion.1), custom_call_target="InvertDiagBlocksLowerTriangular" | custom-call | tf_op jit(solution)/shard_map/jit(_solve_triangular)/triangular_solve | solution.py:71
  918.4 0.2 convolution_bitcast_fusion.2
  918.6 0.6 pad_maximum_fusion
  (36 shorter events, 0.7 us)
Async XLA Ops:
  6.5 3.5 copy-start
  6.5 156.3 %all-reduce.18.cloned.1.call-start = ((), (), s32[]{:S(2)}) async-start(), calls=%async_computation.9 | async-start | bytes 2097152 | tf_op jit(solution)/shard_map/psum | solution.py:43
  11.0 2.2 copy-start.2
  12.0 77.5 %copy-start.1 = (s32[2,128]{1,0:T(2,128)S(1)}, s32[2,128]{1,0:T(2,128)}, u32[]{:S(2)}) copy-start(s32[2,128]{1,0:T(2,128)} %param.13) | copy-start | bytes 3076
  13.2 185.3 %reduce-scatter.7.cloned.1.call-start = ((), (), s32[]{:S(2)}) async-start(), calls=%async_computation.7 | async-start | bytes 147456 | tf_op jit(solution)/shard_map/reduce_scatter | solution.py:51
  165.2 99.7 %all-reduce.8.cloned.1.call-start = ((), (), s32[]{:S(2)}) async-start(), calls=%async_computation.2 | async-start | bytes 131072 | tf_op jit(solution)/shard_map/psum | solution.py:69
  200.7 205.5 %all-reduce.10.cloned.1.call-start = ((), (), s32[]{:S(2)}) async-start(), calls=%async_computation.3 | async-start | bytes 131072 | tf_op jit(solution)/shard_map/psum | solution.py:69
  264.9 177.6 %reduce-scatter.9.cloned.1.call-start = ((), (), s32[]{:S(2)}) async-start(), calls=%async_computation.8 | async-start | bytes 147456 | tf_op jit(solution)/shard_map/reduce_scatter | solution.py:51
  267.2 423.4 %all-reduce.12.cloned.1.call-start = ((), (), s32[]{:S(2)}) async-start(), calls=%async_computation.4 | async-start | bytes 131072 | tf_op jit(solution)/shard_map/psum | solution.py:62
  432.5 319.7 %all-reduce.14.cloned.1.call-start = ((), (), s32[]{:S(2)}) async-start(), calls=%async_computation.5 | async-start | bytes 131072 | tf_op jit(solution)/shard_map/psum | solution.py:69
  693.0 200.8 %all-reduce.16.cloned.1.call-start = ((), (), s32[]{:S(2)}) async-start(), calls=%async_computation.6 | async-start | bytes 131072 | tf_op jit(solution)/shard_map/psum | solution.py:69
Sparse Core Ops, SparseCore 0:
  13.3 149.5 all-reduce.17
  165.4 33.0 reduce-scatter.6
  200.9 63.9 all-reduce.7
  268.1 138.0 all-reduce.9
  408.6 33.8 reduce-scatter.8
  447.9 242.6 all-reduce.11
  693.1 59.0 all-reduce.13
  755.6 138.0 all-reduce.15

commit v2 on v0

--- a/solution.py
+++ b/solution.py
@@ -40,7 +40,7 @@
     for panel in range(panels):
         chosen = wanted[panel * width : (panel + 1) * width]
         old_pivot = (
-            lax.psum(pick_rows(old_vectors, chosen, block_first), "rows")
+            jnp.sum(lax.all_gather(pick_rows(old_vectors, chosen, block_first), "rows"), axis=0)
             .astype(jnp.float32)
             .astype(jnp.bfloat16)
         )

time: 1000 us -> 1130 us (1.13)
  waiting for transfers between devices: 840 us -> 949 us
  other arithmetic: 53.6 us -> 72 us
    all_gather x0 -> x2, waiting for transfers between devices: none -> 189 us  [shards(): lax.all_gather(pick_rows(old_vectors, chosen, block_first), 'rows')]
    psum x1 -> x0, waiting for transfers between devices: 70.1 us -> none  [shards(): lax.psum(pick_rows(old_vectors, chosen, block_first), 'rows')]
    reduce_sum x0 -> x2, other arithmetic: none -> 17.7 us  [shards(): jnp.sum(lax.all_gather(pick_rows(old_vectors, chosen, block_first), 'rows...]
  transfers between devices with their start and end apart: 6 -> 7, of which waited for: 6 -> 7; matrix products, arithmetic and copies ran while one was open for 3% -> 5% of each run, Pallas kernels for 0% -> 0%
where the time goes in v2:
time: 1130 us
  waiting for transfers between devices  949 us (84%)
  blocking collectives  74.5 us (7%)
  other arithmetic  72 us (6%)
  local copies, waits for them, and re-layouts  15.7 us (1%)
  between operations  13.7 us (1%)
    psum x2, waiting for transfers between devices, shards(): block = lax.psum(pick_rows(current, chosen, share_first), ('rows', 'vecs'))  485 us
    psum x1, waiting for transfers between devices, shards(): lax.psum(pick_rows(stacked, chosen, share_first), ('rows', 'vecs'))  248 us
    all_gather x2, waiting for transfers between devices, shards(): lax.all_gather(pick_rows(old_vectors, chosen, block_first), 'rows')  189 us
    all_gather x1, blocking collectives, shards(): every_point = lax.all_gather(coords, ('rows', 'vecs'), axis=1, tiled=True)  74.5 us
    reduce_scatter x2, waiting for transfers between devices, shards(): lax.psum_scatter(residual_term(jnp.int32(0), share * lax.axis_size('vecs'...  26 us
    another operation x6, other arithmetic, shards(): factor = jnp.linalg.cholesky(block)  24.8 us
  transfers between devices with their start and end apart: 7, of which 7 were waited for; matrix products, arithmetic and copies ran while one was open for 5% of the time, Pallas kernels for 0%

profile of v2, /device:TPU:1, one launch (start us, length us, event | category | flops | bytes accessed | tf_op | source)
XLA Modules:
  0.0 1127.6 jit_solution(4638145909487737025)
XLA Ops:
  6.5 0.8 compare_select_fusion.1
  7.3 2.0 gather_fusion
  9.3 0.7 compare_and_fusion.7
  10.0 0.9 gather_fusion.2
  11.0 1.0 select_select_fusion.1
  12.0 0.9 gather_fusion.4
  13.0 1.0 select_select_fusion
  14.0 74.5 %all-gather.2 = f32[256,32,3]{1,2,0:T(4,128)S(1)} all-gather(f32[1,32,3]{1,2,0:T(4,128)} %bitcast.70), channel_id=1, replica_groups=mesh['rows'=32,'vecs'=8] {'rows','vecs'}, dimensions={0}, use_global_device_ids=true | all-gather | bytes 98688 | tf_op jit(solution)/shard_map/all_gather | solution.py:37
  88.5 3.1 copy.23
  91.6 2.9 gather_fusion.1
  94.6 0.3 slice_reduce_fusion.2
  94.9 60.0 %all-gather.6.cloned.1.call-done = bf16[4096,2048]{1,0:T(8,128)(2,1)} async-done(((bf16[128,2048]{1,0:T(8,128)(2,1)}), bf16[4096,2048]{1,0:T(8,128)(2,1)}) %all-gather.6.cloned.1.call-update) | async-done | bytes 16777232 | tf_op jit(solution)/shard_map/all_gather | solution.py:43
  155.0 8.9 reduce_sum.24
  163.8 0.5 convolution_bitcast_fusion.1
  164.3 0.7 copy.31
  165.2 129.2 %all-gather.8.cloned.1.call-done = bf16[4096,2048]{1,0:T(8,128)(2,1)} async-done(((bf16[128,2048]{1,0:T(8,128)(2,1)}), bf16[4096,2048]{1,0:T(8,128)(2,1)}) %all-gather.8.cloned.1.call-update) | async-done | bytes 16777232 | tf_op jit(solution)/shard_map/all_gather | solution.py:43
  294.4 8.9 reduce_sum.25
  303.2 22.6 %reduce-scatter.7.cloned.1.call-done = f32[32,128]{1,0:T(8,128)} async-done(((f32[256,128]{1,0:T(8,128)}), f32[32,128]{1,0:T(8,128)}) %reduce-scatter.7.cloned.1.call-update) | async-done | bytes 16400 | tf_op jit(solution)/shard_map/reduce_scatter | solution.py:51
  325.9 0.8 add_subtract_fusion
  326.7 0.6 gather_fusion.3
  327.4 0.6 select_select_fusion.6
  328.1 0.5 convolution_bitcast_fusion
  328.6 0.7 copy.33
  329.4 0.2 all-reduce.6.cloned.1.call-start
  329.6 244.4 %all-reduce.4.cloned.1.call-done = f32[128,128]{0,1:T(8,128)} async-done(((f32[128,128]{0,1:T(8,128)}), f32[128,128]{0,1:T(8,128)}) %all-reduce.4.cloned.1.call-update) | async-done | bytes 65552 | tf_op jit(solution)/shard_map/psum | solution.py:69
  574.0 0.9 copy.26
  574.9 0.9 fusion.6
  575.8 11.7 %cholesky.44 = f32[128,128]{1,0:T(8,128)S(1)} custom-call(f32[128,128]{1,0:T(8,128)S(1)} %fusion.6), custom_call_target="Cholesky" | custom-call | tf_op jit(solution)/shard_map/jit(cholesky)/cholesky | solution.py:70
  587.5 0.6 compare_reduce_fusion.1
  588.1 0.7 fusion
  588.8 9.8 custom-call.6
  598.6 0.2 fusion.4
  598.8 0.7 gather_fusion.5
  599.5 0.6 select_select_fusion.5
  600.2 0.3 all-reduce.8.cloned.1.call-start
  600.5 3.4 reduce-scatter.9.cloned.1.call-done
  603.8 248.1 %all-reduce.6.cloned.1.call-done = f32[128,128]{0,1:T(8,128)} async-done(((f32[128,128]{0,1:T(8,128)}), f32[128,128]{0,1:T(8,128)}) %all-reduce.6.cloned.1.call-update) | async-done | bytes 65552 | tf_op jit(solution)/shard_map/psum | solution.py:62
  851.9 1.0 convolution_subtract_fusion
  852.9 0.6 gather_fusion.6
  853.7 0.6 select_select_fusion.4
  854.3 241.0 %all-reduce.8.cloned.1.call-done = f32[128,128]{0,1:T(8,128)} async-done(((f32[128,128]{0,1:T(8,128)}), f32[128,128]{0,1:T(8,128)}) %all-reduce.8.cloned.1.call-update) | async-done | bytes 65552 | tf_op jit(solution)/shard_map/psum | solution.py:69
  1095.3 0.9 copy.30
  1096.2 0.9 fusion.3
  1097.1 11.7 %cholesky.55 = f32[128,128]{1,0:T(8,128)S(1)} custom-call(f32[128,128]{1,0:T(8,128)S(1)} %fusion.3), custom_call_target="Cholesky" | custom-call | tf_op jit(solution)/shard_map/jit(cholesky)/cholesky | solution.py:70
  1108.8 0.6 compare_reduce_fusion
  1109.5 0.7 fusion.1
  1110.1 9.8 custom-call.7
  1120.1 0.6 pad_maximum_fusion
  (36 shorter events, 1.0 us)
Async XLA Ops:
  6.5 3.5 copy-start
  6.5 85.0 %copy-start.1 = (s32[2,128]{1,0:T(2,128)S(1)}, s32[2,128]{1,0:T(2,128)}, u32[]{:S(2)}) copy-start(s32[2,128]{1,0:T(2,128)} %param.13) | copy-start | bytes 3076
  6.5 148.4 %all-gather.6.cloned.1.call-start = ((), (), s32[]{:S(2)}) async-start(), calls=%async_computation.5 | async-start | bytes 17301504 | tf_op jit(solution)/shard_map/all_gather | solution.py:43
  11.0 154.2 %copy-start.2 = (f32[3,32]{1,0:T(4,128)S(1)}, f32[3,32]{1,0:T(4,128)}, u32[]{:S(2)}) copy-start(f32[3,32]{1,0:T(4,128)} %param.11) | copy-start | bytes 1156
  12.0 282.4 %all-gather.8.cloned.1.call-start = ((), (), s32[]{:S(2)}) async-start(), calls=%async_computation.6 | async-start | bytes 17301504 | tf_op jit(solution)/shard_map/all_gather | solution.py:43
  14.0 311.9 %reduce-scatter.7.cloned.1.call-start = ((), (), s32[]{:S(2)}) async-start(), calls=%async_computation.7 | async-start | bytes 147456 | tf_op jit(solution)/shard_map/reduce_scatter | solution.py:51
  165.1 408.9 %all-reduce.4.cloned.1.call-start = ((), (), s32[]{:S(2)}) async-start(), calls=%async_computation.2 | async-start | bytes 131072 | tf_op jit(solution)/shard_map/psum | solution.py:69
  328.1 275.8 %reduce-scatter.9.cloned.1.call-start = ((), (), s32[]{:S(2)}) async-start(), calls=%async_computation.8 | async-start | bytes 147456 | tf_op jit(solution)/shard_map/reduce_scatter | solution.py:51
  329.4 522.6 %all-reduce.6.cloned.1.call-start = ((), (), s32[]{:S(2)}) async-start(), calls=%async_computation.3 | async-start | bytes 131072 | tf_op jit(solution)/shard_map/psum | solution.py:62
  600.2 495.1 %all-reduce.8.cloned.1.call-start = ((), (), s32[]{:S(2)}) async-start(), calls=%async_computation.4 | async-start | bytes 131072 | tf_op jit(solution)/shard_map/psum | solution.py:69
Sparse Core Ops, SparseCore 0:
  12.1 142.8 all-gather.5
  157.6 136.7 all-gather.7
  296.9 28.9 reduce-scatter.6
  331.2 242.7 all-reduce.3
  576.3 27.4 reduce-scatter.8
  609.2 242.6 all-reduce.5
  857.4 237.8 all-reduce.7
